TPU v7x, 512 devices: a whole 4x8x8 slice. The times are simulated.
512 devices in a mesh: pipe: 8 (over y_hi, core), ctx: 16 (over z, y_lo), dp: 4 (over x).
Axes of the slice: x: 4, y: 8 (y_hi: 4, y_lo: 2; y = y_hi * 2 + y_lo), z: 8, core: 2. Of those that a mesh axis runs over, the one named last changes fastest.
Arguments:
- state: bfloat16 [8, 4, 2048, 1024], P('pipe', 'dp', 'ctx'), may hold values from -36 to 36
- weights: bfloat16 [2, 8, 1024, 256], P(None, 'pipe'), may hold values from -0.1875 to 0.1875
- out_grad: bfloat16 [2, 8, 4, 2048, 1024], P(None, 'pipe', 'dp', 'ctx'), may hold values from -0.59765625 to 0.59765625
- start_span: int32 [8, 4], P(None, 'dp'), may hold values from 0 to 1
- block_order: int32 [32], replicated, may hold values from 0 to 31, each once
Outputs:
- state_out: bfloat16 [8, 4, 2048, 1024], P('pipe', 'dp', 'ctx')
- weight_grads: float32 [2, 8, 1024, 256], P(None, 'pipe')
All inputs are finite; a program needn't handle non-finite values.
Results may differ from a plain program's by a relative error of at most 0.012.
Values may be sent and summed in bfloat16 or wider, within the bound.
No kernel may reach another device: no remote copies, remote signals or barrier semaphores. Data moves between devices by JAX's collectives and lax.ppermute only.
A program may use at most 64 MiB of HBM per device.

v0:
```python
import math
import jax
import jax.numpy as jnp
from jax import lax
from jax.sharding import PartitionSpec as P

EPS = 1e-05


def from_behind(block, axis, distance):
    devices = range(lax.axis_size(axis))
    route = [((i - distance) % len(devices), i) for i in devices]
    return lax.ppermute(block, axis, route)


def rms_scale(values):
    return lax.rsqrt(jnp.mean(values * values, axis=-1, keepdims=True) + EPS)


def token_positions(block_order, seq_total):
    half_count = block_order.shape[0]
    half_len = seq_total // half_count
    row_ids = jnp.arange(seq_total, dtype=jnp.int32)
    selected = (row_ids // half_len)[:, None] == jnp.arange(half_count, dtype=jnp.int32)[None, :]
    block_ids = jnp.sum(jnp.where(selected, block_order[None, :], 0), axis=1)
    return block_ids * half_len + row_ids % half_len


def shards(state, weights, out_grad, start_span, block_order):
    tok_rows = state.shape[2]
    feat_width = state.shape[3]
    head_dim = weights.shape[3] // 2
    head_count = feat_width // head_dim
    group_size = math.gcd(head_count, 4)
    group_count = head_count // group_size
    span_count = weights.shape[0]
    section_count = lax.axis_size("pipe")
    seq_total = tok_rows * lax.axis_size("ctx")
    score_scale = 1.0 / math.sqrt(head_dim)
    all_positions = token_positions(block_order, seq_total)
    own_positions = lax.dynamic_slice_in_dim(
        all_positions, lax.axis_index("ctx") * tok_rows, tok_rows
    )
    causal = all_positions[None, :] <= own_positions[:, None]
    section_index = lax.axis_index("pipe")
    carried = state[0, 0]
    start_column = start_span[:, 0]
    weight_grads = jnp.zeros((span_count, feat_width, 2 * head_dim), jnp.float32)
    for tick_index in range(out_grad.shape[0]):
        anchor = (section_index - tick_index) % section_count
        first_span = jnp.sum(
            jnp.where(jnp.arange(section_count, dtype=jnp.int32) == anchor, start_column, 0)
        )
        span_index = (first_span + (anchor + tick_index) // section_count) % 2
        weight = lax.dynamic_index_in_dim(weights[:, 0], span_index, 0, keepdims=False)
        widened = carried.astype(jnp.float32)
        normed = (widened * rms_scale(widened)).astype(jnp.bfloat16)
        split_heads = widened.reshape(tok_rows, head_count, head_dim)
        queries = (split_heads * rms_scale(split_heads)).astype(jnp.bfloat16)
        projected = jnp.dot(normed, weight, preferred_element_type=jnp.float32)
        key_raw = projected[:, :head_dim]
        key_scale = rms_scale(key_raw)
        key_unit = key_raw * key_scale
        own_rows = jnp.concatenate([key_unit, projected[:, head_dim:]], axis=1).astype(jnp.bfloat16)
        gathered = lax.all_gather(own_rows, "ctx", axis=0, tiled=True)
        key_rows = gathered[:, :head_dim]
        value_rows = gathered[:, head_dim:]
        query_groups = queries.reshape(tok_rows, group_count, group_size, head_dim).transpose(
            1, 0, 2, 3
        )

        def forward_group(query_part):
            scores = (
                jnp.einsum("qhd,kd->hqk", query_part, key_rows, preferred_element_type=jnp.float32)
                * score_scale
            )
            exponent = jnp.where(causal[None], jnp.exp(scores), 0.0)
            total_weight = jnp.sum(exponent, axis=-1, keepdims=True)
            probs = (exponent / total_weight).astype(jnp.bfloat16)
            attended = jnp.einsum(
                "hqk,kd->qhd", probs, value_rows, preferred_element_type=jnp.float32
            )
            return (probs, attended)

        probs, attended = lax.map(forward_group, query_groups)
        output = attended.transpose(1, 0, 2, 3).reshape(tok_rows, feat_width)
        updated = (widened + output * rms_scale(output)).astype(jnp.bfloat16)
        carried = from_behind(updated, "pipe", 1)
        upstream = out_grad[tick_index, 0, 0]
        upstream_groups = upstream.reshape(tok_rows, group_count, group_size, head_dim).transpose(
            1, 0, 2, 3
        )
        row_delta = jnp.sum(upstream_groups.astype(jnp.float32) * attended, axis=-1).transpose(
            0, 2, 1
        )
        key_grad = jnp.zeros((tok_rows * lax.axis_size("ctx"), head_dim), jnp.float32)
        value_grad = jnp.zeros((tok_rows * lax.axis_size("ctx"), head_dim), jnp.float32)
        for head_block in range(group_count):
            prob_part = probs[head_block]
            value_grad = value_grad + jnp.einsum(
                "hqk,qhd->kd",
                prob_part,
                upstream_groups[head_block],
                preferred_element_type=jnp.float32,
            )
            prob_grad = jnp.einsum(
                "qhd,kd->hqk",
                upstream_groups[head_block],
                value_rows,
                preferred_element_type=jnp.float32,
            )
            score_grad = (
                prob_part.astype(jnp.float32)
                * (prob_grad - row_delta[head_block][..., None])
                * score_scale
            ).astype(jnp.bfloat16)
            key_grad = key_grad + jnp.einsum(
                "hqk,qhd->kd",
                score_grad,
                query_groups[head_block],
                preferred_element_type=jnp.float32,
            )
        key_sums = lax.psum_scatter(
            jnp.concatenate([key_grad, value_grad], axis=1).astype(jnp.bfloat16),
            "ctx",
            scatter_dimension=0,
            tiled=True,
        ).astype(jnp.float32)
        key_delta = key_sums[:, :head_dim]
        key_back = key_scale * (
            key_delta - key_unit * jnp.mean(key_delta * key_unit, axis=-1, keepdims=True)
        )
        grad_rows = jnp.concatenate([key_back, key_sums[:, head_dim:]], axis=1).astype(jnp.bfloat16)
        local_grad = lax.dot_general(
            normed, grad_rows, (((0,), (0,)), ((), ())), preferred_element_type=jnp.float32
        )
        span_mask = (jnp.arange(span_count, dtype=jnp.int32) == span_index).astype(jnp.float32)[
            :, None, None
        ]
        masked_grad = span_mask * local_grad
        weight_grads = weight_grads + masked_grad
    weight_grads = lax.psum(weight_grads, ("ctx", "dp"))
    return (carried[None, None], weight_grads[:, None])


def solution(mesh):
    return jax.shard_map(
        shards,
        mesh=mesh,
        in_specs=(
            P("pipe", "dp", "ctx", None),
            P(None, "pipe", None, None),
            P(None, "pipe", "dp", "ctx", None),
            P(None, "dp"),
            P(),
        ),
        out_specs=(P("pipe", "dp", "ctx", None), P(None, "pipe", None, None)),
        check_vma=False,
    )
```

profile of v0, /device:TPU:16, one launch (start us, length us, event | category | flops | bytes accessed | tf_op | source)
XLA Modules:
  0.0 990.2 jit_solution(8186478735265335391)
XLA Ops:
  7.3 1.4 fusion.99
  10.5 1.2 fusion.58
  16.2 74.4 %all-gather.3.cloned.1.call-done = bf16[2048,256]{1,0:T(8,128)(2,1)} async-done(((bf16[128,256]{1,0:T(8,128)(2,1)}), bf16[2048,256]{1,0:T(8,128)(2,1)}) %all-gather.3.cloned.1.call-update) | async-done | bytes 1048592 | tf_op jit(solution)/shard_map/all_gather | solution.py:65
  90.6 1.3 fusion.117
  92.7 2.5 broadcast.232.clone2
  95.2 22.0 %while.26 = (s32[]{:T(128)}, bf16[2,4,128,2048]{2,3,1,0:T(8,128)(2,1)}, f32[2,128,4,128]{3,1,2,0:T(8,128)}, bf16[2,128,4,128]{1,3,2,0:T(8,128)(2,1)}, bf16[2048,...) while((s32[]{:T(128)}, ...), condition=%wide.region_7.8_spmd.clone, body=%wide.region_5.7_spmd.clone.sunk | while | flops 548666880 | bytes 33962720 | solution.py:85
  95.4 2.3 bitcast_reduce_fusion.4
  97.8 1.8 fusion.136
  100.5 2.5 copy.225
  103.0 3.2 constant_dynamic-update-slice_fusion.4
  106.4 2.3 bitcast_reduce_fusion.4
  108.8 1.8 fusion.136
  111.5 2.5 copy.225
  114.0 3.1 constant_dynamic-update-slice_fusion.4
  118.4 1.4 copy.152
  120.1 1.9 collective-permute-start
  122.8 6.8 collective-permute-done
  132.6 1.3 multiply_reduce_fusion.1
  134.4 2.3 convolution_bitcast_fusion.6
  136.7 2.3 fusion.38
  139.0 4.0 convolution_bitcast_fusion.8
  143.1 3.4 fusion.39
  149.1 56.5 %all-gather.5.cloned.1.call-done = bf16[2048,256]{1,0:T(8,128)(2,1)} async-done(((bf16[128,256]{1,0:T(8,128)(2,1)}), bf16[2048,256]{1,0:T(8,128)(2,1)}) %all-gather.5.cloned.1.call-update) | async-done | bytes 1048592 | tf_op jit(solution)/shard_map/all_gather | solution.py:65
  205.6 1.3 fusion.116
  207.7 2.5 broadcast.232.clone
  210.1 22.0 %while.27 = (s32[]{:T(128)}, bf16[2,4,128,2048]{2,3,1,0:T(8,128)(2,1)}, f32[2,128,4,128]{3,1,2,0:T(8,128)}, bf16[2,128,4,128]{1,3,2,0:T(8,128)(2,1)}, bf16[2048,...) while((s32[]{:T(128)}, ...), condition=%wide.region_15.16_spmd.clone, body=%wide.region_13.15_spmd.clone.sunk | while | flops 548666880 | bytes 33962720 | solution.py:85
  210.4 2.3 bitcast_reduce_fusion.5
  212.7 1.8 fusion.140
  215.5 2.5 copy.226
  218.0 3.2 constant_dynamic-update-slice_fusion.5
  221.4 2.3 bitcast_reduce_fusion.5
  223.7 1.8 fusion.140
  226.5 2.5 copy.226
  229.0 3.1 constant_dynamic-update-slice_fusion.5
  232.1 1.4 multiply_reduce_fusion
  233.6 2.3 convolution_bitcast_fusion.2
  235.9 2.3 fusion.36
  238.2 3.9 convolution_bitcast_fusion.4
  242.1 4.0 fusion.37
  246.2 2.2 pad_maximum_fusion.1
  248.4 35.8 %reduce-scatter.3.cloned.1.call-done = bf16[128,256]{1,0:T(8,128)(2,1)} async-done(((bf16[2048,256]{1,0:T(8,128)(2,1)}), bf16[128,256]{1,0:T(8,128)(2,1)}) %reduce-scatter.3.cloned.1.call-update) | async-done | bytes 65552 | tf_op jit(solution)/shard_map/reduce_scatter | solution.py:123
  287.2 73.8 %reduce-scatter.5.cloned.1.call-done = bf16[128,256]{1,0:T(8,128)(2,1)} async-done(((bf16[2048,256]{1,0:T(8,128)(2,1)}), bf16[128,256]{1,0:T(8,128)(2,1)}) %reduce-scatter.5.cloned.1.call-update) | async-done | bytes 65552 | tf_op jit(solution)/shard_map/reduce_scatter | solution.py:123
  363.9 1.7 add_bitcast_fusion
  365.6 1.4 copy.156
  368.5 1.9 collective-permute-start.1
  370.5 7.2 collective-permute-done.1
  377.7 602.2 %all-reduce.2.cloned.1.call-done = f32[2,1,1024,256]{3,2,1,0:T(8,128)} async-done(((f32[2,1,1024,256]{3,2,1,0:T(8,128)}), f32[2,1,1024,256]{3,2,1,0:T(8,128)}) %all-reduce.2.cloned.1.call-update) | async-done | bytes 2097168 | tf_op jit(solution)/shard_map/psum | solution.py:142
  980.6 3.0 copy.256
  (144 shorter events, 27.6 us)
Async XLA Ops:
  7.2 3.3 copy-start
  7.2 8.0 copy-start.23
  7.2 83.4 %all-gather.3.cloned.1.call-start = ((), (), s32[]{:S(2)}) async-start(), calls=%async_computation.2 | async-start | bytes 1114112 | tf_op jit(solution)/shard_map/all_gather | solution.py:65
  10.5 1.4 copy-start.19
  12.6 192.9 %all-gather.5.cloned.1.call-start = ((), (), s32[]{:S(2)}) async-start(), calls=%async_computation.3 | async-start | bytes 1114112 | tf_op jit(solution)/shard_map/all_gather | solution.py:65
  95.2 24.8 %copy-start.1 = (bf16[1,1,128,1024]{3,2,1,0:T(8,128)(2,1)S(1)}, bf16[1,1,128,1024]{3,2,1,0:T(8,128)(2,1)}, u32[]{:S(2)}) copy-start(bf16[1,1,128,1024]{3,2,1,0:T(8,128)(2,1)} %param.9) | copy-start | bytes 786436
  95.2 2.6 copy-start.13
  95.2 2.6 copy-start.15
  103.0 3.2 copy-start.14
  103.0 3.2 copy-start.16
  106.2 2.6 copy-start.13
  106.2 2.6 copy-start.15
  114.0 3.1 copy-start.14
  114.0 3.1 copy-start.16
  117.1 14.0 %copy-start.8 = (bf16[2,1,1,128,1024]{4,3,2,1,0:T(8,128)(2,1)S(1)}, bf16[2,1,1,128,1024]{4,3,2,1,0:T(8,128)(2,1)}, u32[]{:S(2)}) copy-start(bf16[2,1,1,128,1024]{4,3,2,1,0:T(8,128)(2,1)} %param.11) | copy-start | bytes 1572868
  120.1 9.4 collective-permute-start
  129.6 18.6 %copy-start.2 = (bf16[128,1024]{1,0:T(8,128)(2,1)}, bf16[128,1024]{1,0:T(8,128)(2,1)S(1)}, u32[]{:S(2)}) copy-start(bf16[128,1024]{1,0:T(8,128)(2,1)S(1)} %collective-permute-done) | copy-start | bytes 786436
  129.7 0.6 copy-start.21
  130.0 4.4 copy-start.5
  130.3 0.9 copy-start.17
  131.1 153.1 %reduce-scatter.3.cloned.1.call-start = ((), (), s32[]{:S(2)}) async-start(), calls=%async_computation.4 | async-start | bytes 1114112 | tf_op jit(solution)/shard_map/reduce_scatter | solution.py:123
  147.6 213.4 %reduce-scatter.5.cloned.1.call-start = ((), (), s32[]{:S(2)}) async-start(), calls=%async_computation.5 | async-start | bytes 1114112 | tf_op jit(solution)/shard_map/reduce_scatter | solution.py:123
  210.1 2.6 copy-start.9
  210.1 2.6 copy-start.11
  218.0 3.2 copy-start.10
  218.0 3.2 copy-start.12
  221.2 2.6 copy-start.9
  221.2 2.6 copy-start.11
  229.0 3.1 copy-start.10
  229.0 3.1 copy-start.12
  232.1 3.8 copy-start.4
  232.1 6.1 copy-start.7
  242.1 44.6 %copy-start.20 = (f32[128]{0:T(128)S(1)}, f32[128]{0:T(128)}, u32[]{:S(2)}) copy-start(f32[128]{0:T(128)} %copy-done.19) | copy-start | bytes 1540
  246.1 114.8 %copy-start.6 = (f32[128,256]{1,0:T(8,128)S(1)}, f32[128,256]{1,0:T(8,128)}, u32[]{:S(2)}) copy-start(f32[128,256]{1,0:T(8,128)} %copy-done.5) | copy-start | bytes 393220
  246.1 114.8 %copy-start.18 = (f32[128]{0:T(128)S(1)}, f32[128]{0:T(128)}, u32[]{:S(2)}) copy-start(f32[128]{0:T(128)} %copy-done.17) | copy-start | bytes 1540
  246.1 117.4 %copy-start.3 = (bf16[128,1024]{1,0:T(8,128)(2,1)S(1)}, bf16[128,1024]{1,0:T(8,128)(2,1)}, u32[]{:S(2)}) copy-start(bf16[128,1024]{1,0:T(8,128)(2,1)} %copy-done.2) | copy-start | bytes 786436
  246.1 117.4 %copy-start.22 = (f32[128]{0:T(128)S(1)}, f32[128]{0:T(128)}, u32[]{:S(2)}) copy-start(f32[128]{0:T(128)} %copy-done.21) | copy-start | bytes 1540
  248.4 731.6 %all-reduce.2.cloned.1.call-start = ((), (), s32[]{:S(2)}) async-start(), calls=%async_computation.6 | async-start | bytes 4194304 | tf_op jit(solution)/shard_map/psum | solution.py:142
  368.5 9.2 collective-permute-start.1
Sparse Core Ops, SparseCore 0:
  12.8 77.7 all-gather.2
  131.2 74.3 all-gather.4
  208.4 75.7 reduce-scatter.2
  287.7 73.2 reduce-scatter.4
  365.7 614.1 all-reduce.1
where the time goes:
time: 992 us; the launch traced here: 990 us
  waiting for transfers between devices  857 us (86%)
  local copies, waits for them, and re-layouts  44.1 us (4%)
  matrix products  43.5 us (4%)
  other arithmetic  25.8 us (3%)
  between operations  15.7 us (2%)
    psum x1, waiting for transfers between devices, shards(): weight_grads = lax.psum(weight_grads, ('ctx', 'dp'))  602 us
    all_gather x2, waiting for transfers between devices, shards(): gathered = lax.all_gather(own_rows, 'ctx', axis=0, tiled=True)  131 us
    reduce_scatter x2, waiting for transfers between devices, shards(): lax.psum_scatter(jnp.concatenate([key_grad, value_grad], axis=1).astype(j...  110 us
    dynamic_update_slice x8, local copies, waits for them, and re-layouts, shards(): probs, attended = lax.map(forward_group, query_groups)  22.5 us
  transfers between devices with their start and end apart: 7, of which 7 were waited for; matrix products, arithmetic and copies ran while one was open for 7% of the time, Pallas kernels for 0%

commit v1 on v0

--- a/solution.py
+++ b/solution.py
@@ -62,7 +62,10 @@
         key_scale = rms_scale(key_raw)
         key_unit = key_raw * key_scale
         own_rows = jnp.concatenate([key_unit, projected[:, head_dim:]], axis=1).astype(jnp.bfloat16)
-        gathered = lax.all_gather(own_rows, "ctx", axis=0, tiled=True)
+        gathered = jnp.concatenate(
+            lax.all_to_all(jnp.stack([own_rows for _ in range(lax.axis_size("ctx"))]), "ctx", 0, 0),
+            0,
+        )
         key_rows = gathered[:, :head_dim]
         value_rows = gathered[:, head_dim:]
         query_groups = queries.reshape(tok_rows, group_count, group_size, head_dim).transpose(

time: 992 us -> 899 us (0.906)
  waiting for transfers between devices: 857 us -> 743 us
  starting transfers between devices: 4.23 us -> 22.3 us
    all_gather x2 -> x0, waiting for transfers between devices: 131 us -> none  [shards(): gathered = lax.all_gather(own_rows, 'ctx', axis=0, tiled=True)]
    all_to_all x0 -> x2, waiting for transfers between devices: none -> 32.1 us  [shards(): lax.all_to_all(jnp.stack([own_rows for _ in range(lax.axis_size('ctx'))])...]
    all_to_all x0 -> x2, starting transfers between devices: none -> 18.2 us  [shards(): lax.all_to_all(jnp.stack([own_rows for _ in range(lax.axis_size('ctx'))])...]
    reduce_scatter x2, waiting for transfers between devices: 110 us -> 99 us  [shards(): lax.psum_scatter(jnp.concatenate([key_grad, value_grad], axis=1).astype(j...]
  transfers between devices with their start and end apart: 7 -> 7, of which waited for: 7 -> 7; matrix products, arithmetic and copies ran while one was open for 7% -> 8% of each run, Pallas kernels for 0% -> 0%
where the time goes in v1:
time: 899 us; the launch traced here: 898 us
  waiting for transfers between devices  743 us (83%)
  local copies, waits for them, and re-layouts  49.8 us (6%)
  matrix products  43.5 us (5%)
  other arithmetic  23.6 us (3%)
  starting transfers between devices  22.3 us (2%)
  between operations  15.7 us (2%)
    psum x1, waiting for transfers between devices, shards(): weight_grads = lax.psum(weight_grads, ('ctx', 'dp'))  602 us
    reduce_scatter x2, waiting for transfers between devices, shards(): lax.psum_scatter(jnp.concatenate([key_grad, value_grad], axis=1).astype(j...  99 us
    all_to_all x2, waiting for transfers between devices, shards(): lax.all_to_all(jnp.stack([own_rows for _ in range(lax.axis_size('ctx'))])...  32.1 us
    dynamic_update_slice x8, local copies, waits for them, and re-layouts, shards(): probs, attended = lax.map(forward_group, query_groups)  22.6 us
    all_to_all x2, starting transfers between devices, shards(): lax.all_to_all(jnp.stack([own_rows for _ in range(lax.axis_size('ctx'))])...  18.2 us
  transfers between devices with their start and end apart: 7, of which 7 were waited for; matrix products, arithmetic and copies ran while one was open for 8% of the time, Pallas kernels for 0%

profile of v1, /device:TPU:16, one launch (start us, length us, event | category | flops | bytes accessed | tf_op | source)
XLA Modules:
  0.0 897.8 jit_solution(17873652809544849672)
XLA Ops:
  7.2 1.4 fusion.99
  13.6 11.6 %all-to-all-start = ((bf16[16,128,256]{2,1,0:T(8,128)(2,1)}), bf16[16,128,256]{2,1,0:T(8,128)(2,1)S(1)}, u32[]{:S(2)}, u32[]{:S(2)}) async-start(bf16[16,128,256]{2,1,0:T(8,128)(2,1)} %stack.4), calls=%async_computation | async-start | bytes 2097152 | tf_op jit(solution)/shard_map/all_to_all | solution.py:66
  27.9 1.8 fusion.118
  33.6 19.2 %all-to-all-done = bf16[16,128,256]{2,1,0:T(8,128)(2,1)S(1)} async-done(((bf16[16,128,256]{2,1,0:T(8,128)(2,1)}), bf16[16,128,256]{2,1,0:T(8,128)(2,1)S(1)}, u32[]{:S(2)}, u32[]{:S(2)}) %all-to-all-start) | async-done | bytes 1048608 | tf_op jit(solution)/shard_map/all_to_all | solution.py:66
  53.9 2.5 broadcast.234.clone2
  56.4 22.0 %while.26 = (s32[]{:T(128)}, bf16[2,4,128,2048]{2,3,1,0:T(8,128)(2,1)}, f32[2,128,4,128]{3,1,2,0:T(8,128)}, bf16[2,128,4,128]{1,3,2,0:T(8,128)(2,1)}, bf16[2048,...) while((s32[]{:T(128)}, ...), condition=%wide.region_7.8_spmd.clone, body=%wide.region_5.7_spmd.clone.sunk | while | flops 548666880 | bytes 33962720 | solution.py:88
  56.6 2.3 bitcast_reduce_fusion.4
  59.0 1.8 fusion.136
  61.7 2.5 copy.225
  64.2 3.2 constant_dynamic-update-slice_fusion.4
  67.6 2.3 bitcast_reduce_fusion.4
  70.0 1.8 fusion.136
  72.7 2.5 copy.225
  75.2 3.1 constant_dynamic-update-slice_fusion.4
  79.6 1.4 copy.152
  81.3 1.9 collective-permute-start
  83.2 1.3 multiply_reduce_fusion.1
  84.6 3.3 convolution_bitcast_fusion.6
  87.9 2.1 collective-permute-done
  92.7 6.6 all-to-all-start.1
  100.1 3.3 fusion.38
  103.5 4.0 convolution_bitcast_fusion.8
  107.5 4.0 fusion.39
  111.5 2.3 pad_maximum_fusion
  114.5 12.9 %all-to-all-done.1 = bf16[16,128,256]{2,1,0:T(8,128)(2,1)} async-done(((bf16[16,128,256]{2,1,0:T(8,128)(2,1)}), bf16[16,128,256]{2,1,0:T(8,128)(2,1)}, u32[]{:S(2)}, u32[]{:S(2)}) %all-to-all-start.1) | async-done | bytes 1048608 | tf_op jit(solution)/shard_map/all_to_all | solution.py:66
  127.4 1.3 fusion.116
  129.5 2.5 broadcast.234.clone
  132.0 19.9 %while.27 = (s32[]{:T(128)}, bf16[2,4,128,2048]{2,3,1,0:T(8,128)(2,1)}, f32[2,128,4,128]{3,1,2,0:T(8,128)}, bf16[2,128,4,128]{1,3,2,0:T(8,128)(2,1)S(1)}, bf16[2...) while((s32[]{:T(128)}, ...), condition=%wide.region_15.16_spmd.clone, body=%wide.region_13.15_spmd.clone.sunk | while | flops 548666880 | bytes 36059928 | solution.py:88
  133.5 1.8 fusion.140
  136.2 2.5 copy.226
  138.7 3.2 constant_dynamic-update-slice_fusion.5
  142.2 1.3 bitcast_reduce_fusion.5
  143.5 1.8 fusion.140
  146.2 2.5 copy.226
  148.7 3.1 constant_dynamic-update-slice_fusion.5
  151.9 1.4 multiply_reduce_fusion
  153.4 2.3 convolution_bitcast_fusion.2
  155.7 2.3 fusion.36
  158.0 4.1 convolution_bitcast_fusion.4
  162.2 3.3 fusion.37
  166.7 25.3 %reduce-scatter.3.cloned.1.call-done = bf16[128,256]{1,0:T(8,128)(2,1)} async-done(((bf16[2048,256]{1,0:T(8,128)(2,1)}), bf16[128,256]{1,0:T(8,128)(2,1)}) %reduce-scatter.3.cloned.1.call-update) | async-done | bytes 65552 | tf_op jit(solution)/shard_map/reduce_scatter | solution.py:126
  194.9 73.7 %reduce-scatter.5.cloned.1.call-done = bf16[128,256]{1,0:T(8,128)(2,1)} async-done(((bf16[2048,256]{1,0:T(8,128)(2,1)}), bf16[128,256]{1,0:T(8,128)(2,1)}) %reduce-scatter.5.cloned.1.call-update) | async-done | bytes 65552 | tf_op jit(solution)/shard_map/reduce_scatter | solution.py:126
  271.6 1.7 add_bitcast_fusion
  273.3 1.4 copy.156
  276.2 1.9 collective-permute-start.1
  278.2 7.5 collective-permute-done.1
  285.6 601.9 %all-reduce.2.cloned.1.call-done = f32[2,1,1024,256]{3,2,1,0:T(8,128)} async-done(((f32[2,1,1024,256]{3,2,1,0:T(8,128)}), f32[2,1,1024,256]{3,2,1,0:T(8,128)}) %all-reduce.2.cloned.1.call-update) | async-done | bytes 2097168 | tf_op jit(solution)/shard_map/psum | solution.py:145
  888.2 3.0 copy.256
  (164 shorter events, 32.9 us)
Async XLA Ops:
  7.2 3.2 copy-start
  7.2 18.6 %copy-start.1 = (bf16[1,1,128,1024]{3,2,1,0:T(8,128)(2,1)S(1)}, bf16[1,1,128,1024]{3,2,1,0:T(8,128)(2,1)}, u32[]{:S(2)}) copy-start(bf16[1,1,128,1024]{3,2,1,0:T(8,128)(2,1)} %param.9) | copy-start | bytes 786436
  10.4 3.2 copy-start.26
  11.8 0.6 copy-start.22
  13.5 19.1 %copy-start.31 = (s32[32]{0:T(128)S(1)}, s32[32]{0:T(128)}, u32[]{:S(2)}) copy-start(s32[32]{0:T(128)} %param.13) | copy-start | bytes 388
  13.6 39.3 %all-to-all-start = ((bf16[16,128,256]{2,1,0:T(8,128)(2,1)}), bf16[16,128,256]{2,1,0:T(8,128)(2,1)S(1)}, u32[]{:S(2)}, u32[]{:S(2)}) async-start(bf16[16,128,256]{2,1,0:T(8,128)(2,1)} %stack.4), calls=%async_computation | async-start | bytes 2097152 | tf_op jit(solution)/shard_map/all_to_all | solution.py:66
  52.9 3.5 copy-start.4
  56.4 2.6 copy-start.14
  56.4 2.6 copy-start.16
  64.2 3.2 copy-start.15
  64.2 3.2 copy-start.17
  67.4 2.6 copy-start.14
  67.4 2.6 copy-start.16
  75.2 3.1 copy-start.15
  75.2 3.1 copy-start.17
  78.3 6.2 copy-start.7
  81.3 8.7 collective-permute-start
  90.0 24.3 %copy-start.2 = (bf16[128,1024]{1,0:T(8,128)(2,1)}, bf16[128,1024]{1,0:T(8,128)(2,1)S(1)}, u32[]{:S(2)}) copy-start(bf16[128,1024]{1,0:T(8,128)(2,1)S(1)} %collective-permute-done) | copy-start | bytes 786436
  90.1 13.4 %copy-start.5 = (bf16[16,128,256]{2,1,0:T(8,128)(2,1)S(1)}, bf16[16,128,256]{2,1,0:T(8,128)(2,1)}, u32[]{:S(2)}) copy-start(bf16[16,128,256]{2,1,0:T(8,128)(2,1)} %copy-done.4) | copy-start | bytes 3145732
  90.4 0.7 copy-start.8
  91.1 0.5 copy-start.24
  92.7 34.7 %all-to-all-start.1 = ((bf16[16,128,256]{2,1,0:T(8,128)(2,1)}), bf16[16,128,256]{2,1,0:T(8,128)(2,1)}, u32[]{:S(2)}, u32[]{:S(2)}) async-start(bf16[16,128,256]{2,1,0:T(8,128)(2,1)} %stack.5), calls=%async_computation.1 | async-start | bytes 2097152 | tf_op jit(solution)/shard_map/all_to_all | solution.py:66
  99.3 92.6 %reduce-scatter.3.cloned.1.call-start = ((), (), s32[]{:S(2)}) async-start(), calls=%async_computation.4 | async-start | bytes 1114112 | tf_op jit(solution)/shard_map/reduce_scatter | solution.py:126
  103.5 4.0 copy-start.30
  113.8 154.8 %reduce-scatter.5.cloned.1.call-start = ((), (), s32[]{:S(2)}) async-start(), calls=%async_computation.5 | async-start | bytes 1114112 | tf_op jit(solution)/shard_map/reduce_scatter | solution.py:126
  132.0 1.5 copy-start.10
  132.0 1.5 copy-start.12
  132.0 1.5 copy-start.18
  138.7 3.2 copy-start.11
  138.7 3.2 copy-start.13
  138.7 3.2 copy-start.19
  141.9 1.5 copy-start.10
  142.0 1.5 copy-start.12
  142.0 1.5 copy-start.18
  148.7 3.1 copy-start.11
  148.7 3.1 copy-start.13
  148.7 3.1 copy-start.19
  151.9 1.5 copy-start.20
  151.9 3.8 copy-start.6
  153.4 4.7 copy-start.21
  162.1 30.5 %copy-start.23 = (f32[128]{0:T(128)S(1)}, f32[128]{0:T(128)}, u32[]{:S(2)}) copy-start(f32[128]{0:T(128)} %copy-done.22) | copy-start | bytes 1540
  162.1 32.3 %copy-start.27 = (f32[128]{0:T(128)S(1)}, f32[128]{0:T(128)}, u32[]{:S(2)}) copy-start(f32[128]{0:T(128)} %copy-done.26) | copy-start | bytes 1540
  165.5 103.2 %copy-start.9 = (f32[128,256]{1,0:T(8,128)S(1)}, f32[128,256]{1,0:T(8,128)}, u32[]{:S(2)}) copy-start(f32[128,256]{1,0:T(8,128)} %copy-done.8) | copy-start | bytes 393220
  165.5 103.2 %copy-start.25 = (f32[128]{0:T(128)S(1)}, f32[128]{0:T(128)}, u32[]{:S(2)}) copy-start(f32[128]{0:T(128)} %copy-done.24) | copy-start | bytes 1540
  165.5 105.7 %copy-start.3 = (bf16[128,1024]{1,0:T(8,128)(2,1)S(1)}, bf16[128,1024]{1,0:T(8,128)(2,1)}, u32[]{:S(2)}) copy-start(bf16[128,1024]{1,0:T(8,128)(2,1)} %copy-done.2) | copy-start | bytes 786436
  165.5 105.7 %copy-start.29 = (f32[128]{0:T(128)S(1)}, f32[128]{0:T(128)}, u32[]{:S(2)}) copy-start(f32[128]{0:T(128)} %copy-done.28) | copy-start | bytes 1540
  166.6 720.9 %all-reduce.2.cloned.1.call-start = ((), (), s32[]{:S(2)}) async-start(), calls=%async_computation.6 | async-start | bytes 4194304 | tf_op jit(solution)/shard_map/psum | solution.py:145
  276.2 9.4 %collective-permute-start.1 = (bf16[128,1024]{1,0:T(8,128)(2,1)S(1)}, bf16[128,1024]{1,0:T(8,128)(2,1)S(1)}, u32[]{:S(2)}, u32[]{:S(2)}) collective-permute-start(bf16[128,1024]{1,0:T(8,128)(2,1)S(1)} %add_convert_fusion), channel_id=1, source_target_pairs={{448,0},{0,64},{64,128},{128,192},{192,256},{256,320},{320,384},{3... | collective-permute-start | bytes 786440 | tf_op jit(solution)/shard_map/ppermute | solution.py:13
  (1 other events, 0.5 us)
Sparse Core Ops, SparseCore 0:
  114.0 77.9 reduce-scatter.2
  195.5 73.0 reduce-scatter.4
  273.4 614.0 all-reduce.1
